TPU v7x, 32 devices: a whole 2x2x4 slice. The times are simulated.
32 devices in a mesh: member: 4 (over y, core), lon: 4 (over z), lat: 2 (over x).
Axes of the slice: x: 2, y: 2, z: 4, core: 2. Of those that a mesh axis runs over, the one named last changes fastest.
Arguments:
- member_state: float32 [4, 16, 256, 1536], P('member', None, 'lat', 'lon'), may hold values from -12 to 12
- column_depth: float32 [256, 1536], P('lat', 'lon'), may hold values from 0.5 to 2
- rotation: float32 [256, 1536], P('lat', 'lon'), may hold values from -0.2 to 0.2
- diffusivity: float32 [5, 256, 1536], P(None, 'lat', 'lon'), may hold values from 0.02 to 0.2
- ocean_mask: int32 [256, 1536], P('lat', 'lon'), may hold values from 0 to 1, as said below
- region_id: int32 [256, 1536], P('lat', 'lon'), may hold values from 0 to 15, as said below
- target_rms: float32 [16], replicated, may hold values from 0.2 to 1
Outputs:
- bred_state: float32 [4, 16, 256, 1536], P('member', None, 'lat', 'lon')
- growth_rms: float32 [4, 16], P('member')
Inputs may be any that keep to these rules, and one draw needn't show every extreme that they name: `ocean_mask`: 1 marks an ocean cell. `region_id`: every region id holds ocean cells.
All inputs are finite; a program needn't handle non-finite values.
Results may differ from a plain program's by a relative error of at most 0.0003.
Values sent between devices are 32-bit elements; how exact they have to be, the bound alone decides.
A program may use at most 64 MiB of HBM per device.

v0:
```python
import jax
import jax.numpy as jnp
from jax import lax
from jax.sharding import PartitionSpec as P

LEV = 5
STEPS = 2


divergence_gain = 0.25
pressure_gain = 0.25
buoyancy_gain = 0.1
advection_gain = 0.05
epsilon = 1e-06


def padded_2(cells, sides, width):
    for axis, dim in sides:
        count = lax.axis_size(axis)
        head = lax.slice_in_dim(cells, 0, width, axis=dim)
        tail = lax.slice_in_dim(cells, cells.shape[dim] - width, cells.shape[dim], axis=dim)
        cells = jnp.concatenate(
            [
                lax.ppermute(tail, axis, [(i, (i + 1) % count) for i in range(count)]),
                cells,
                lax.ppermute(head, axis, [((i + 1) % count, i) for i in range(count)]),
            ],
            axis=dim,
        )
    return cells


def spread(value, axis, source):
    kept = jnp.where(lax.axis_index(axis) == source, value, 0).astype(value.dtype)
    return lax.psum(kept, axis)


def inside_rows(count, margin):
    rows = jnp.arange(count + 2 * margin)
    global_row = lax.axis_index("lat") * count + rows - margin
    total_rows = lax.axis_size("lat") * count
    inside = (global_row >= 0) & (global_row < total_rows)
    return jnp.where(inside, 1.0, 0.0).astype(jnp.float32)[:, None]


def sides(padded):
    return (
        padded[..., 1:-1, 2:],
        padded[..., 1:-1, :-2],
        padded[..., 2:, 1:-1],
        padded[..., :-2, 1:-1],
    )


def inner_one(field):
    return field[..., 1:-1, 1:-1]


def shrink_step(state, coefs):
    centre = inner_one(state)
    east_side, west_side, north_side, south_side = sides(state)
    zonal_diff = east_side - west_side
    merid_diff = north_side - south_side
    laplacian = east_side + west_side + north_side + south_side - 4.0 * centre
    first = inner_one(coefs)
    divergence = jnp.mean(zonal_diff[:, 1 : 1 + LEV], axis=1) + jnp.mean(
        merid_diff[:, 1 + LEV : 1 + 2 * LEV], axis=1
    )
    new_surface = first[2] * (centre[:, 0] - divergence_gain * first[0] * divergence)
    s_east, s_west, s_north, s_south = sides(new_surface)
    slope_east = (s_east - s_west)[:, None]
    slope_north = (s_north - s_south)[:, None]
    second = inner_one(first)
    rotation = second[1]
    ocean_float = second[2]
    diffusivity = second[3:]
    inner_state = inner_one(centre)
    zonal_flow = inner_state[:, 1 : 1 + LEV]
    merid_flow = inner_state[:, 1 + LEV : 1 + 2 * LEV]
    heat_field = inner_state[:, 1 + 2 * LEV :]
    inner_lap = inner_one(laplacian)
    heat_east = inner_one(zonal_diff[:, 1 + 2 * LEV :])
    heat_north = inner_one(merid_diff[:, 1 + 2 * LEV :])
    new_zonal = ocean_float * (
        zonal_flow
        + rotation * merid_flow
        - pressure_gain * slope_east
        - buoyancy_gain * heat_east
        + diffusivity * inner_lap[:, 1 : 1 + LEV]
    )
    new_merid = ocean_float * (
        merid_flow
        - rotation * zonal_flow
        - pressure_gain * slope_north
        - buoyancy_gain * heat_north
        + diffusivity * inner_lap[:, 1 + LEV : 1 + 2 * LEV]
    )
    new_heat = ocean_float * (
        heat_field
        + diffusivity * inner_lap[:, 1 + 2 * LEV :]
        - advection_gain * (new_zonal * heat_east + new_merid * heat_north)
    )
    return jnp.concatenate(
        [new_surface[:, None, 1:-1, 1:-1], new_zonal, new_merid, new_heat], axis=1
    )


def run_steps(state, column_depth, rotation, diffusivity, ocean_float):
    members, channels, rows, columns = state.shape
    margin = 2 * STEPS
    coefs = jnp.concatenate(
        [column_depth[None], rotation[None], ocean_float[None], diffusivity], axis=0
    )
    stacked = jnp.concatenate([state.reshape(members * channels, rows, columns), coefs], axis=0)
    padded = padded_2(stacked, (("lon", 2), ("lat", 1)), margin) * inside_rows(rows, margin)
    field = padded[: members * channels].reshape(
        members, channels, rows + 2 * margin, columns + 2 * margin
    )
    coef_pad = padded[members * channels :]
    for step_index in range(STEPS):
        crop = 2 * step_index
        coef_now = coef_pad[:, crop : rows + 2 * margin - crop, crop : columns + 2 * margin - crop]
        field = shrink_step(field, coef_now)
    return field


def per_device(
    member_state, column_depth, rotation, diffusivity, ocean_mask, region_id, target_rms
):
    ocean_float = ocean_mask.astype(jnp.float32)
    channels = member_state.shape[1]
    labels = jnp.arange(target_rms.shape[0])
    onehot = (region_id[None] == labels[:, None, None]).astype(jnp.float32)
    local_counts = jnp.einsum("rji,ji->r", onehot, ocean_float, precision=lax.Precision.HIGHEST)
    state = member_state
    state = run_steps(state, column_depth, rotation, diffusivity, ocean_float)
    control = spread(state, "member", 0)
    difference = state - control
    cell_sum = ocean_float * jnp.sum(difference * difference, axis=1)[0]
    local_squares = jnp.einsum("rji,ji->r", onehot, cell_sum, precision=lax.Precision.HIGHEST)
    squares, counts = lax.psum((local_squares, local_counts), ("lon", "lat"))
    growth = jnp.sqrt(squares / (counts * channels) + epsilon)
    factor = target_rms / growth
    cell_factor = jnp.einsum("r,rji->ji", factor, onehot, precision=lax.Precision.HIGHEST)
    bred = control + cell_factor * difference
    return (bred, growth[None])


def solution(mesh):
    return jax.shard_map(
        per_device,
        mesh=mesh,
        in_specs=(
            P("member", None, "lat", "lon"),
            P("lat", "lon"),
            P("lat", "lon"),
            P(None, "lat", "lon"),
            P("lat", "lon"),
            P("lat", "lon"),
            P(),
        ),
        out_specs=(P("member", None, "lat", "lon"), P("member", None)),
        check_vma=False,
    )
```

profile of v0, /device:TPU:0, one launch (start us, length us, event | category | flops | bytes accessed | tf_op | source)
XLA Modules:
  0.0 186.6 jit_solution(10231089591109092940)
XLA Ops:
  7.2 0.0 copy-start.10
  7.2 0.0 all-reduce.3.cloned.1.call-start
  7.2 2.2 %bitcast_dynamic-update-slice_fusion = f32[24,128,384]{2,1,0:T(8,128)S(1)} fusion(f32[1,16,128,384]{3,2,1,0:T(8,128)} %param.7), kind=kLoop, calls=%fused_computation.14 | loop fusion | bytes 6291456
  9.6 0.0 copy-done.6
  9.6 0.0 copy-done.7
  9.6 0.1 constant_dynamic-update-slice_fusion
  9.7 0.6 fusion.39
  10.3 1.5 copy-done
  11.8 0.5 copy.17
  12.3 3.1 %collective-permute-start = (f32[24,128,4]{1,0,2:T(8,128)S(1)}, f32[24,128,4]{1,0,2:T(8,128)S(1)}, u32[]{:S(2)}, u32[]{:S(2)}) collective-permute-start(f32[24,128,4]{1,0,2:T(8,128)S(1)} %copy.17), channel_id=1, source_target_pairs={{0,2},{2,4},{4,6},{6,0},{1,3},{3,5},{5,7},{7,1},{8,10},{10,12},{12... | collective-permute-start | bytes 147464 | tf_op jit(solution)/shard_map/ppermute | solution.py:24
  15.4 0.5 copy.18
  15.8 2.1 %collective-permute-start.1 = (f32[24,128,4]{1,0,2:T(8,128)S(1)}, f32[24,128,4]{1,0,2:T(8,128)S(1)}, u32[]{:S(2)}, u32[]{:S(2)}) collective-permute-start(f32[24,128,4]{1,0,2:T(8,128)S(1)} %copy.18), channel_id=1, source_target_pairs={{2,0},{4,2},{6,4},{0,6},{3,1},{5,3},{7,5},{1,7},{10,8},{12,10},{14... | collective-permute-start | bytes 147464 | tf_op jit(solution)/shard_map/ppermute | solution.py:26
  17.9 1.6 collective-permute-done
  19.5 0.5 copy.19
  20.0 0.1 collective-permute-done.1
  20.1 0.5 copy.20
  20.6 2.1 %pad_maximum_fusion.4 = (f32[24,4,392]{2,1,0:T(4,128)}, f32[24,4,392]{2,1,0:T(4,128)}) fusion(f32[24,128,4]{2,1,0:T(8,128)S(1)} %copy.20, f32[24,128,384]{2,1,0:T(8,128)} %copy-done, f32[24,128,4]{2,1,0:T(8,128)S(1)} %copy.19), kind=kLoop, calls=%fused_computation.78 | loop fusion | flops 150528 | bytes 5117952 | tf_op jit(solution)/shard_map/slice | solution.py:21
  22.8 1.7 collective-permute-start.2
  24.5 0.3 collective-permute-start.3
  24.8 5.9 %collective-permute-done.2 = f32[24,4,392]{2,1,0:T(4,128)S(1)} collective-permute-done((f32[24,4,392]{2,1,0:T(4,128)}, f32[24,4,392]{2,1,0:T(4,128)S(1)}, u32[]{:S(2)}, u32[]{:S(2)}) %collective-permute-start.2) | collective-permute-done | bytes 150560 | tf_op jit(solution)/shard_map/ppermute | solution.py:24
  30.7 3.0 %collective-permute-done.3 = f32[24,4,392]{2,1,0:T(4,128)} collective-permute-done((f32[24,4,392]{2,1,0:T(4,128)}, f32[24,4,392]{2,1,0:T(4,128)}, u32[]{:S(2)}, u32[]{:S(2)}) %collective-permute-start.3) | collective-permute-done | bytes 150560 | tf_op jit(solution)/shard_map/ppermute | solution.py:26
  33.8 5.1 %maximum_multiply_fusion = f32[24,136,392]{2,1,0:T(8,128)S(1)} fusion(f32[24,4,392]{2,1,0:T(4,128)} %collective-permute-done.3, f32[24,128,4]{2,1,0:T(8,128)S(1)} %copy.20, f32[24,128,384]{2,1,0:T(8,128)} %copy-done, f32[24,128,4]{2,1,0:T(8,128)S(1)} %copy.19, f32[24,4,392]{2,1,0:T(4,128)S(1)} %collective-permute-done.2, f32[136]{0:T(256)S(1)} %and_select_fusion), kind=kLoop, calls=%fused_computation | loop fusion | flops 6397440 | bytes 10236448 | tf_op jit(solution)/shard_map/mul | solution.py:115
  38.9 0.5 slice_bitcast_fusion
  39.5 1.1 slice_bitcast_fusion.3
  40.5 0.8 slice_bitcast_fusion.8
  41.4 6.9 %slice_subtract_fusion.3 = (f32[1,16,134,390]{3,2,1,0:T(8,128)}, f32[1,16,134,390]{3,2,1,0:T(8,128)}, f32[1,16,134,390]{3,2,1,0:T(8,128)S(1)}) fusion(f32[1,16,136,392]{3,2,1,0:T(8,128)S(1)} %slice_bitcast_fusion), kind=kLoop, calls=%fused_computation.10 | loop fusion | flops 5853120 | bytes 26757120 | tf_op jit(solution)/shard_map/sub | solution.py:62
  48.2 2.2 %slice_reduce_fusion.2 = (f32[134,390]{1,0:T(8,128)S(1)}, f32[134,390]{1,0:T(8,128)S(1)}) fusion(f32[1,16,134,390]{3,2,1,0:T(8,128)} %get-tuple-element.26, f32[1,16,134,390]{3,2,1,0:T(8,128)} %get-tuple-element.25), kind=kLoop, calls=%fused_computation.35 | loop fusion | flops 418080 | bytes 2508480 | tf_op jit(solution)/shard_map/reduce_sum | solution.py:66
  50.4 0.3 fusion.29
  50.7 1.0 slice_bitcast_fusion.6
  51.7 7.1 %fusion.8 = (f32[1,5,132,388]{3,2,1,0:T(8,128)S(1)}, f32[1,5,132,388]{3,2,1,0:T(8,128)S(1)}, f32[1,5,132,388]{3,2,1,0:T(8,128)}) fusion(f32[1,16,134,390]{3,2,1,0:T(8,128)S(1)} %get-tuple-element.27, f32[1,16,136,392]{3,2,1,0:T(8,128)S(1)} %slice_bitcast_fusion, f32[1,16,134,390]{3,2,1,0:T(8,128)} %get-tuple-element.26, ...), kind=kLoop, calls=%fused_computation.27 | loop fusion | flops 6145920 | bytes 13111296 | tf_op jit(solution)/shard_map/mul | solution.py:98
  58.8 2.9 %pad_maximum_fusion = f32[1,16,132,388]{3,2,1,0:T(8,128)S(1)} fusion(f32[1,5,132,388]{3,2,1,0:T(8,128)S(1)} %get-tuple-element.11, f32[1,5,132,388]{3,2,1,0:T(8,128)} %get-tuple-element.13, f32[1,5,132,388]{3,2,1,0:T(8,128)S(1)} %get-tuple-element.12, f32[1,1,132,388]{3,2,1,0:T(8,128)S(1)} %get-tuple-element.31), kind=kLoop, calls=%fused_computation.6 | loop fusion | flops 2458368 | bytes 6555648 | tf_op jit(solution)/shard_map/concatenate | solution.py:103
  61.7 7.1 %slice_subtract_fusion.1 = (f32[1,16,130,386]{3,2,1,0:T(8,128)}, f32[1,16,130,386]{3,2,1,0:T(8,128)S(1)}, f32[1,16,130,386]{3,2,1,0:T(8,128)}) fusion(f32[1,16,132,388]{3,2,1,0:T(8,128)S(1)} %pad_maximum_fusion), kind=kLoop, calls=%fused_computation.8 | loop fusion | flops 5620160 | bytes 25692160 | tf_op jit(solution)/shard_map/sub | solution.py:62
  68.8 1.7 slice_reduce_fusion
  70.5 1.5 slice_reduce_fusion.1
  72.0 0.3 fusion.26
  72.4 0.3 slice_bitcast_fusion.10
  72.7 4.7 %fusion.15 = (f32[1,5,128,384]{3,2,1,0:T(8,128)S(1)}, f32[1,5,128,384]{3,2,1,0:T(8,128)S(1)}, f32[1,5,128,384]{3,2,1,0:T(8,128)S(1)}) fusion(f32[1,16,130,386]{3,2,1,0:T(8,128)S(1)} %get-tuple-element.23, f32[1,5,132,388]{3,2,1,0:T(8,128)S(1)} %copy-done.2, f32[1,16,130,386]{3,2,1,0:T(8,128)} %get-tuple-element.24, ...), kind=kLoop, calls=%fused_computation.40 | loop fusion | flops 5898240 | bytes 12582912 | tf_op jit(solution)/shard_map/mul | solution.py:98
  77.4 1.9 %fusion.5 = f32[1,16,128,384]{3,2,1,0:T(8,128)} fusion(f32[1,5,128,384]{3,2,1,0:T(8,128)S(1)} %get-tuple-element.8, f32[1,5,128,384]{3,2,1,0:T(8,128)S(1)} %get-tuple-element.10, f32[1,5,128,384]{3,2,1,0:T(8,128)S(1)} %get-tuple-element.9, f32[1,1,128,384]{3,2,1,0:T(8,128)S(1)} %get-tuple-element.28, pred[]{:T(512)S(6)} %eq.16), kind=kLoop, calls=%fused_computation.21 | loop fusion | flops 3145728 | bytes 6291457 | tf_op jit(solution)/shard_map/jit(_where)/select_n | solution.py:34
  79.3 0.0 all-reduce.3.cloned.1.call-update
  79.3 2.3 %iota_compare_fusion = pred[16,128,384]{2,1,0:T(32,128)(4,1)} fusion(s32[128,384]{1,0:T(8,128)} %param.12), kind=kLoop, calls=%fused_computation.17 | loop fusion | flops 786432 | bytes 983040 | tf_op jit(solution)/shard_map/eq | solution.py:133
  81.6 66.6 %all-reduce.3.cloned.1.call-done = f32[1,16,128,384]{3,2,1,0:T(8,128)} async-done(((f32[1,16,128,384]{3,2,1,0:T(8,128)}), f32[1,16,128,384]{3,2,1,0:T(8,128)}) %all-reduce.3.cloned.1.call-update) | async-done | bytes 3145744 | tf_op jit(solution)/shard_map/psum | solution.py:35
  148.2 2.4 %multiply_reduce_fusion = f32[128,384]{1,0:T(8,128)S(1)} fusion(f32[1,16,128,384]{3,2,1,0:T(8,128)} %all-reduce.3.cloned.1.call-done, f32[1,5,128,384]{3,2,1,0:T(8,128)S(1)} %get-tuple-element.8, f32[1,5,128,384]{3,2,1,0:T(8,128)S(1)} %get-tuple-element.10, f32[1,5,128,384]{3,2,1,0:T(8,128)S(1)} %get-tuple-element.9, f32[1,1,128,384]{3,2,1,0:T(8,128)S(1)} %get-tuple-element.28), kind=kLoop, calls=%fused_computation.16 | loop fusion | flops 4669440 | bytes 6488064 | tf_op jit(solution)/shard_map/reduce_sum | solution.py:139
  150.6 0.0 copy-done.8
  150.6 0.8 select_reduce_fusion
  151.4 21.3 %all-reduce = (f32[16]{0:T(128)S(1)}, f32[16]{0:T(128)S(1)}) all-reduce(f32[16]{0:T(128)S(1)} %get-tuple-element.5, f32[16]{0:T(128)S(1)} %get-tuple-element.4), channel_id=1, replica_groups=mesh['member'=4,'lon'=4,'lat'=2] {'lon','lat'}, use_global_device_ids=true, to_apply=%region_6.7 | all-reduce | flops 32 | bytes 256 | tf_op jit(solution)/shard_map/psum | solution.py:141
  172.8 0.5 fusion.34
  173.3 2.4 %fusion.2 = f32[1,128,384]{2,0,1:T(1,128)S(1)} fusion(pred[16,128,384]{2,1,0:T(32,128)(4,1)} %iota_compare_fusion, f32[16]{0:T(128)S(1)} %copy-done.12, f32[16]{0:T(128)S(1)} %get-tuple-element.6, f32[16]{0:T(128)S(1)} %get-tuple-element.7), kind=kOutput, calls=%fused_computation.18 | convolution fusion | flops 9437248 | bytes 983232 | tf_op jit(solution)/shard_map/r,rji->ji/dot_general | solution.py:144
  175.7 4.0 %multiply_add_fusion = f32[1,16,128,384]{3,2,1,0:T(8,128)} fusion(f32[1,16,128,384]{3,2,1,0:T(8,128)} %all-reduce.3.cloned.1.call-done, f32[1,5,128,384]{3,2,1,0:T(8,128)S(1)} %get-tuple-element.8, f32[1,5,128,384]{3,2,1,0:T(8,128)S(1)} %get-tuple-element.10, f32[1,5,128,384]{3,2,1,0:T(8,128)S(1)} %get-tuple-element.9, ...), kind=kLoop, calls=%fused_computation.15 | loop fusion | flops 4718592 | bytes 9633792 | tf_op jit(solution)/shard_map/add | solution.py:145
  (28 shorter events, 0.2 us)
Async XLA Ops:
  7.2 2.3 %copy-start.10 = (f32[128,384]{1,0:T(8,128)S(1)}, f32[128,384]{1,0:T(8,128)}, u32[]{:S(2)}) copy-start(f32[128,384]{1,0:T(8,128)} %param.8) | copy-start | bytes 589828
  7.2 2.3 %copy-start.11 = (f32[128,384]{1,0:T(8,128)S(1)}, f32[128,384]{1,0:T(8,128)}, u32[]{:S(2)}) copy-start(f32[128,384]{1,0:T(8,128)} %param.9) | copy-start | bytes 589828
  7.2 2.4 %copy-start.6 = (s32[128,384]{1,0:T(8,128)S(1)}, s32[128,384]{1,0:T(8,128)}, u32[]{:S(2)}) copy-start(s32[128,384]{1,0:T(8,128)} %param.11) | copy-start | bytes 589828
  7.2 2.4 %copy-start.7 = (f32[5,128,384]{2,1,0:T(8,128)S(1)}, f32[5,128,384]{2,1,0:T(8,128)}, u32[]{:S(2)}) copy-start(f32[5,128,384]{2,1,0:T(8,128)} %param.10) | copy-start | bytes 2949124
  7.2 141.0 %all-reduce.3.cloned.1.call-start = ((), (), s32[]{:S(2)}) async-start(), calls=%async_computation | async-start | bytes 6291456 | tf_op jit(solution)/shard_map/psum | solution.py:35
  9.7 2.1 %copy-start = (f32[24,128,384]{2,1,0:T(8,128)}, f32[24,128,384]{2,1,0:T(8,128)S(1)}, u32[]{:S(2)}) copy-start(f32[24,128,384]{2,1,0:T(8,128)S(1)} %constant_dynamic-update-slice_fusion) | copy-start | bytes 14155780
  12.3 7.2 %collective-permute-start = (f32[24,128,4]{1,0,2:T(8,128)S(1)}, f32[24,128,4]{1,0,2:T(8,128)S(1)}, u32[]{:S(2)}, u32[]{:S(2)}) collective-permute-start(f32[24,128,4]{1,0,2:T(8,128)S(1)} %copy.17), channel_id=1, source_target_pairs={{0,2},{2,4},{4,6},{6,0},{1,3},{3,5},{5,7},{7,1},{8,10},{10,12},{12... | collective-permute-start | bytes 147464 | tf_op jit(solution)/shard_map/ppermute | solution.py:24
  15.8 4.3 %collective-permute-start.1 = (f32[24,128,4]{1,0,2:T(8,128)S(1)}, f32[24,128,4]{1,0,2:T(8,128)S(1)}, u32[]{:S(2)}, u32[]{:S(2)}) collective-permute-start(f32[24,128,4]{1,0,2:T(8,128)S(1)} %copy.18), channel_id=1, source_target_pairs={{2,0},{4,2},{6,4},{0,6},{3,1},{5,3},{7,5},{1,7},{10,8},{12,10},{14... | collective-permute-start | bytes 147464 | tf_op jit(solution)/shard_map/ppermute | solution.py:26
  22.8 8.0 %collective-permute-start.2 = (f32[24,4,392]{2,1,0:T(4,128)}, f32[24,4,392]{2,1,0:T(4,128)S(1)}, u32[]{:S(2)}, u32[]{:S(2)}) collective-permute-start(f32[24,4,392]{2,1,0:T(4,128)} %get-tuple-element.14), channel_id=1, source_target_pairs={{0,1},{1,0},{2,3},{3,2},{4,5},{5,4},{6,7},{7,6},{8,9},{9,8},{10,11... | collective-permute-start | bytes 451592 | tf_op jit(solution)/shard_map/ppermute | solution.py:24
  24.5 9.3 %collective-permute-start.3 = (f32[24,4,392]{2,1,0:T(4,128)}, f32[24,4,392]{2,1,0:T(4,128)}, u32[]{:S(2)}, u32[]{:S(2)}) collective-permute-start(f32[24,4,392]{2,1,0:T(4,128)} %get-tuple-element.15), channel_id=1, source_target_pairs={{1,0},{0,1},{3,2},{2,3},{5,4},{4,5},{7,6},{6,7},{9,8},{8,9},{11,10... | collective-permute-start | bytes 451592 | tf_op jit(solution)/shard_map/ppermute | solution.py:26
  58.8 2.9 %copy-start.1 = (f32[1,5,132,388]{3,2,1,0:T(8,128)}, f32[1,5,132,388]{3,2,1,0:T(8,128)S(1)}, u32[]{:S(2)}) copy-start(f32[1,5,132,388]{3,2,1,0:T(8,128)S(1)} %get-tuple-element.11) | copy-start | bytes 3072964
  58.8 2.9 %copy-start.3 = (f32[1,5,132,388]{3,2,1,0:T(8,128)}, f32[1,5,132,388]{3,2,1,0:T(8,128)S(1)}, u32[]{:S(2)}) copy-start(f32[1,5,132,388]{3,2,1,0:T(8,128)S(1)} %get-tuple-element.12) | copy-start | bytes 3072964
  68.8 3.8 %copy-start.2 = (f32[1,5,132,388]{3,2,1,0:T(8,128)S(1)}, f32[1,5,132,388]{3,2,1,0:T(8,128)}, u32[]{:S(2)}) copy-start(f32[1,5,132,388]{3,2,1,0:T(8,128)} %copy-done.1) | copy-start | bytes 3072964
  68.8 3.8 %copy-start.4 = (f32[1,5,132,388]{3,2,1,0:T(8,128)S(1)}, f32[1,5,132,388]{3,2,1,0:T(8,128)}, u32[]{:S(2)}) copy-start(f32[1,5,132,388]{3,2,1,0:T(8,128)} %copy-done.3) | copy-start | bytes 3072964
  68.8 3.8 %copy-start.5 = (f32[1,5,132,388]{3,2,1,0:T(8,128)S(1)}, f32[1,5,132,388]{3,2,1,0:T(8,128)}, u32[]{:S(2)}) copy-start(f32[1,5,132,388]{3,2,1,0:T(8,128)} %get-tuple-element.13) | copy-start | bytes 3072964
  68.8 3.9 %copy-start.9 = (f32[128,384]{1,0:T(8,128)S(1)}, f32[128,384]{1,0:T(8,128)}, u32[]{:S(2)}) copy-start(f32[128,384]{1,0:T(8,128)} %get-tuple-element.17) | copy-start | bytes 589828
  81.6 91.7 %copy-start.12 = (f32[16]{0:T(128)S(1)}, f32[16]{0:T(128)}, u32[]{:S(2)}) copy-start(f32[16]{0:T(128)} %param.13) | copy-start | bytes 196
  148.2 2.4 %copy-start.8 = (s32[128,384]{1,0:T(8,128)S(1)}, s32[128,384]{1,0:T(8,128)}, u32[]{:S(2)}) copy-start(s32[128,384]{1,0:T(8,128)} %param.12) | copy-start | bytes 589828
Sparse Core Ops, SparseCore 0:
  79.4 68.7 all-reduce.2
where the time goes:
time: 187 us
  waiting for transfers between devices  77.3 us (41%)
  other arithmetic  55.1 us (29%)
  blocking collectives  21.3 us (11%)
  between operations  14.3 us (8%)
  local copies, waits for them, and re-layouts  8.9 us (5%)
  starting transfers between devices  7.2 us (4%)
  matrix products  2.38 us (1%)
    psum x1, waiting for transfers between devices, spread(): return lax.psum(kept, axis)  66.6 us
    psum x1, blocking collectives, per_device(): squares, counts = lax.psum((local_squares, local_counts), ('lon', 'lat'))  21.3 us
    sub x2, other arithmetic, shrink_step(): zonal_diff = east_side - west_side  13.9 us
    mul x2, other arithmetic, shrink_step(): ocean_float * (heat_field + diffusivity * inner_lap[:, 1 + 2 * LEV:] - ad...  11.8 us
    ppermute x2, waiting for transfers between devices, padded_2(): lax.ppermute(tail, axis, [(i, (i + 1) % count) for i in range(count)])  7.55 us
    mul x1, other arithmetic, run_steps(): padded_2(stacked, (('lon', 2), ('lat', 1)), margin)  5.14 us
    ppermute x2, starting transfers between devices, padded_2(): lax.ppermute(tail, axis, [(i, (i + 1) % count) for i in range(count)])  4.79 us
    add x1, other arithmetic, per_device(): bred = control + cell_factor * difference  3.99 us
  transfers between devices with their start and end apart: 5, of which 5 were waited for; matrix products, arithmetic and copies ran while one was open for 2% of the time, Pallas kernels for 0%

commit v1 on v0

v1 whole, which is shorter than its diff:
```python
import functools

import jax
import jax.numpy as jnp
from jax import lax
from jax.experimental import pallas as pl
from jax.experimental.pallas import tpu as pltpu
from jax.sharding import PartitionSpec as P

LEV = 5
STEPS = 2
MARGIN = 2 * STEPS
TILE = 8
LANES = 128

divergence_gain = 0.25
pressure_gain = 0.25
buoyancy_gain = 0.1
advection_gain = 0.05
epsilon = 1e-06

MESH = pl.DeviceIdType.MESH


def chunk_tiles(rows):
    tiles = rows // TILE
    return 2 if tiles % 2 == 0 else 1


def cycle_kernel(
    sizes,
    state_in, depth_in, rotation_in, diffusivity_in, mask_in, region_in,
    own_out, control_out, growth_out,
    field, middle, own, control, mask, region, surface, merid_sum,
    send_east, send_west, from_east, from_west,
    send_north, send_south, from_north, from_south,
    squares, counts, gathered,
    in_sem, halo_send, halo_recv, cast_send, cast_recv, out_sem, sum_send, sum_recv,
):
    members, lons, lats = sizes
    channels, rows, columns = state_in.shape
    regions = growth_out.shape[0]
    fields = field.shape[0]
    wide = columns + LANES
    tiles = rows // TILE
    per_chunk = chunk_tiles(rows)
    chunk_rows = per_chunk * TILE
    chunks = rows // chunk_rows
    DEPTH, ROT, OCEAN, DIFF = channels, channels + 1, channels + 2, channels + 3

    me = lax.axis_index("member")
    lon = lax.axis_index("lon")
    lat = lax.axis_index("lat")

    def at(dlat, dlon):
        return {
            "member": me,
            "lon": lax.rem(lon + dlon + lons, lons),
            "lat": lax.rem(lat + dlat + lats, lats),
        }

    def to_member(other):
        return {"member": other, "lon": lon, "lat": lat}

    inner = (slice(TILE, TILE + rows), slice(0, columns))
    loads = [
        pltpu.make_async_copy(state_in, field.at[(slice(0, channels),) + inner], in_sem.at[0]),
        pltpu.make_async_copy(depth_in, field.at[(DEPTH,) + inner], in_sem.at[1]),
        pltpu.make_async_copy(rotation_in, field.at[(ROT,) + inner], in_sem.at[2]),
        pltpu.make_async_copy(diffusivity_in, field.at[(slice(DIFF, fields),) + inner], in_sem.at[3]),
        pltpu.make_async_copy(mask_in, mask, in_sem.at[4]),
        pltpu.make_async_copy(region_in, region, in_sem.at[5]),
    ]
    for load in loads:
        load.start()

    peers = [(a, b) for a in range(lats) for b in range(lons) if (a, b) != (0, 0)]
    barrier = pltpu.get_barrier_semaphore()
    for a, b in peers:
        pl.semaphore_signal(barrier, inc=1, device_id=at(a, b), device_id_type=MESH)
    even = lax.rem(me, 2) == 0
    has_pair = even & (me + 1 < members)
    has_next = even & (me + 2 < members)
    parent = jnp.where(even, me - 2, me - 1)

    @pl.when(me > 0)
    def _():
        pl.semaphore_signal(barrier, inc=1, device_id=to_member(parent), device_id_type=MESH)

    pl.semaphore_wait(
        barrier, len(peers) + has_pair.astype(jnp.int32) + has_next.astype(jnp.int32)
    )

    for load in loads:
        load.wait()

    lane = lax.broadcasted_iota(jnp.int32, (TILE, LANES), 1)
    sub = lax.broadcasted_iota(jnp.int32, (TILE, columns), 0)
    zero_tile = jnp.zeros((TILE, LANES), jnp.float32)

    def make_ocean(t, carry):
        r = pl.multiple_of(t * TILE, TILE)
        field[OCEAN, pl.ds(r + TILE, TILE), 0:columns] = mask[pl.ds(r, TILE), :].astype(jnp.float32)
        return carry

    lax.fori_loop(0, tiles, make_ocean, 0)

    for k in range(fields // 2):
        a, b = 2 * k, 2 * k + 1
        top = slice(rows, rows + TILE)
        low = slice(TILE, 2 * TILE)
        half = TILE // 2
        send_north[k] = jnp.where(
            sub < half, pltpu.roll(field[a, top, 0:columns], half, 0), field[b, top, 0:columns]
        )
        send_south[k] = jnp.where(
            sub < half, field[a, low, 0:columns], pltpu.roll(field[b, low, 0:columns], half, 0)
        )

    def remote(src, dst, index, device):
        return pltpu.make_async_remote_copy(
            src_ref=src, dst_ref=dst, send_sem=halo_send.at[index], recv_sem=halo_recv.at[index],
            device_id=device, device_id_type=MESH,
        )

    has_north = lat < lats - 1
    has_south = lat > 0
    whole = slice(TILE, TILE + rows)
    last = slice(rows - TILE, rows)
    first = slice(0, TILE)
    above = slice(rows + TILE, rows + 2 * TILE)
    north = [remote(send_north, from_south, 0, at(1, 0))]
    south = [remote(send_south, from_north, 1, at(-1, 0))]
    sideways = [
        remote(send_east, from_west.at[whole], 2, at(0, 1)),
        remote(send_west, from_east.at[whole], 3, at(0, -1)),
    ]
    north_corners = [
        remote(send_east.at[last], from_west.at[first], 4, at(1, 1)),
        remote(send_west.at[last], from_east.at[first], 5, at(1, -1)),
    ]
    south_corners = [
        remote(send_east.at[first], from_west.at[above], 6, at(-1, 1)),
        remote(send_west.at[first], from_east.at[above], 7, at(-1, -1)),
    ]

    @pl.when(has_north)
    def _():
        for copy in north:
            copy.start()

    @pl.when(has_south)
    def _():
        for copy in south:
            copy.start()

    def pack(t, carry):
        r = pl.multiple_of(t * TILE, TILE)
        east, west = zero_tile, zero_tile
        for f in range(fields):
            here = (lane >= MARGIN * f) & (lane < MARGIN * (f + 1))
            edge = field[f, pl.ds(r + TILE, TILE), columns - LANES : columns]
            east = jnp.where(here, pltpu.roll(edge, (MARGIN * f + MARGIN) % LANES, 1), east)
            edge = field[f, pl.ds(r + TILE, TILE), 0:LANES]
            west = jnp.where(here, pltpu.roll(edge, MARGIN * f, 1) if f else edge, west)
        send_east[pl.ds(r, TILE), :] = east
        send_west[pl.ds(r, TILE), :] = west
        return carry

    lax.fori_loop(0, tiles, pack, 0)
    for copy in sideways:
        copy.start()

    @pl.when(has_north)
    def _():
        for copy in north_corners:
            copy.start()

    @pl.when(has_south)
    def _():
        for copy in south_corners:
            copy.start()

    def clear(ref):
        for k in range(regions):
            ref[k] = zero_tile

    def add_regions(ref, r, value):
        ids = region[pl.ds(r, TILE), :]
        for k in range(regions):
            picked = jnp.where(ids == k, value, 0.0)
            total = picked[:, 0:LANES]
            for c in range(LANES, columns, LANES):
                total = total + picked[:, c : c + LANES]
            ref[k] = ref[k] + total

    def share(ref, which):
        gathered[which, 0] = jnp.sum(ref[...], axis=1)
        for p, (a, b) in enumerate(peers):
            pltpu.make_async_remote_copy(
                src_ref=gathered.at[which, 0], dst_ref=gathered.at[which, p + 1],
                send_sem=sum_send.at[which, p], recv_sem=sum_recv.at[which, p],
                device_id=at(a, b), device_id_type=MESH,
            ).start()

    def collect(which):
        for p, (a, b) in enumerate(peers):
            pltpu.make_async_remote_copy(
                src_ref=gathered.at[which, 0], dst_ref=gathered.at[which, p + 1],
                send_sem=sum_send.at[which, p], recv_sem=sum_recv.at[which, p],
                device_id=at(a, b), device_id_type=MESH,
            ).wait()
        total = gathered[which, 0]
        for p in range(len(peers)):
            total = total + gathered[which, p + 1]
        return jnp.sum(total, axis=1, keepdims=True)

    clear(squares)
    clear(counts)

    def count(t, carry):
        r = pl.multiple_of(t * TILE, TILE)
        add_regions(counts, r, field[OCEAN, pl.ds(r + TILE, TILE), 0:columns])
        return carry

    lax.fori_loop(0, tiles, count, 0)
    share(counts, 0)

    for copy in sideways:
        copy.wait()

    @pl.when(has_north)
    def _():
        for copy in north + north_corners:
            copy.wait_send()
        for copy in south + south_corners:
            copy.wait_recv()

    @pl.when(has_south)
    def _():
        for copy in south + south_corners:
            copy.wait_send()
        for copy in north + north_corners:
            copy.wait_recv()

    @pl.when(jnp.logical_not(has_north))
    def _():
        from_north[...] = jnp.zeros_like(from_north)
        from_east[above, :] = zero_tile
        from_west[above, :] = zero_tile

    @pl.when(jnp.logical_not(has_south))
    def _():
        from_south[...] = jnp.zeros_like(from_south)
        from_east[first, :] = zero_tile
        from_west[first, :] = zero_tile

    for k in range(fields // 2):
        a, b = 2 * k, 2 * k + 1
        field[a, first, 0:columns] = pltpu.roll(from_south[k], TILE // 2, 0)
        field[b, first, 0:columns] = from_south[k]
        field[a, above, 0:columns] = from_north[k]
        field[b, above, 0:columns] = pltpu.roll(from_north[k], TILE // 2, 0)

    def unpack(t, carry):
        r = pl.multiple_of(t * TILE, TILE)
        east = from_east[pl.ds(r, TILE), :]
        west = from_west[pl.ds(r, TILE), :]
        for f in range(fields):
            to_first = pltpu.roll(east, LANES - MARGIN * f, 1) if f else east
            to_last = pltpu.roll(west, LANES - MARGIN - MARGIN * f, 1)
            field[f, pl.ds(r, TILE), columns:wide] = jnp.where(lane < MARGIN, to_first, to_last)
        return carry

    lax.fori_loop(0, tiles + 2, unpack, 0)

    sub_wide = lax.broadcasted_iota(jnp.int32, (TILE, wide), 0)

    def starts(t):
        r = pl.multiple_of(t * TILE, TILE)
        before = pl.multiple_of(jnp.maximum(t - 1, 0) * TILE, TILE)
        after = pl.multiple_of(jnp.minimum(t + 1, tiles + 1) * TILE, TILE)
        return r, before, after

    def east_west(q, width):
        return (
            pltpu.roll(q, wide - 1, 1)[:, 0:width],
            pltpu.roll(q, 1, 1)[:, 0:width],
        )

    def north_south(q, below, beyond):
        rows_of = sub_wide[:, 0 : q.shape[1]]
        return (
            pltpu.roll(jnp.where(rows_of == 0, beyond, q), TILE - 1, 0),
            pltpu.roll(jnp.where(rows_of == TILE - 1, below, q), 1, 0),
        )

    def add_up(ref, base, r):
        total = ref[base, pl.ds(r, TILE), :]
        for k in range(1, LEV):
            total = total + ref[base + k, pl.ds(r, TILE), :]
        return total

    def merid_pass(src):
        def body(t, carry):
            r = pl.multiple_of(t * TILE, TILE)
            merid_sum[pl.ds(r, TILE), :] = add_up(src, 1 + LEV, r)
            return carry

        lax.fori_loop(0, tiles + 2, body, 0)

    def surface_pass(src):
        def body(t, carry):
            r, before, after = starts(t)
            e, w = east_west(add_up(src, 1, r), wide)
            n, s = north_south(
                merid_sum[pl.ds(r, TILE), :],
                merid_sum[pl.ds(before, TILE), :],
                merid_sum[pl.ds(after, TILE), :],
            )
            divergence = (e - w) + (n - s)
            now = pl.ds(r, TILE)
            surface[now, :] = field[OCEAN, now, :] * (
                src[0, now, :] - (divergence_gain / LEV) * field[DEPTH, now, :] * divergence
            )
            return carry

        lax.fori_loop(0, tiles + 2, body, 0)

    def update_tile(src, t, width, write):
        r, before, after = starts(t)
        now, below, beyond = pl.ds(r, TILE), pl.ds(before, TILE), pl.ds(after, TILE)

        def around(ref, *index):
            whole_q = ref[(*index, now, slice(None))]
            q = whole_q[:, 0:width]
            e, w = east_west(whole_q, width)
            n, s = north_south(
                q, ref[(*index, below, slice(0, width))], ref[(*index, beyond, slice(0, width))]
            )
            return q, e, w, n, s

        new_surface, e, w, n, s = around(surface)
        slope_east = pressure_gain * (e - w)
        slope_north = pressure_gain * (n - s)
        ocean = field[OCEAN, now, 0:width]
        rotation = field[ROT, now, 0:width]
        write(0, r, new_surface)
        for k in range(LEV):
            mixing = field[DIFF + k, now, 0:width]
            u, ue, uw, un, us = around(src, 1 + k)
            v, ve, vw, vn, vs = around(src, 1 + LEV + k)
            c, ce, cw, cn, cs = around(src, 1 + 2 * LEV + k)
            heat_east = ce - cw
            heat_north = cn - cs
            new_u = ocean * (
                u + rotation * v - slope_east - buoyancy_gain * heat_east
                + mixing * (((ue + uw) + (un + us)) - 4.0 * u)
            )
            new_v = ocean * (
                v - rotation * u - slope_north - buoyancy_gain * heat_north
                + mixing * (((ve + vw) + (vn + vs)) - 4.0 * v)
            )
            new_c = ocean * (
                c + mixing * (((ce + cw) + (cn + cs)) - 4.0 * c)
                - advection_gain * (new_u * heat_east + new_v * heat_north)
            )
            write(1 + k, r, new_u)
            write(1 + LEV + k, r, new_v)
            write(1 + 2 * LEV + k, r, new_c)

    merid_pass(field)
    surface_pass(field)

    def first_step(t, carry):
        def write(channel, r, value):
            middle[channel, pl.ds(r, TILE), :] = value

        update_tile(field, t, wide, write)
        return carry

    lax.fori_loop(0, tiles + 2, first_step, 0)
    merid_pass(middle)
    surface_pass(middle)

    def cast(c, which, device):
        part = control.at[:, pl.ds(pl.multiple_of(c * chunk_rows, TILE), chunk_rows), :]
        return pltpu.make_async_remote_copy(
            src_ref=part, dst_ref=part, send_sem=cast_send.at[which, c], recv_sem=cast_recv.at[c],
            device_id=to_member(device), device_id_type=MESH,
        )

    def pass_on(c):
        @pl.when(has_next)
        def _():
            cast(c, 1, me + 2).start()

        @pl.when(has_pair)
        def _():
            cast(c, 0, me + 1).start()

    def save(c, which):
        part = pl.ds(pl.multiple_of(c * chunk_rows, TILE), chunk_rows)
        src, dst = (own, own_out) if which == 0 else (control, control_out)
        return pltpu.make_async_copy(src.at[:, part, :], dst.at[:, part, :], out_sem.at[which, c])

    def second_step(c, carry):
        def one(j, inner_carry):
            def write(channel, r, value):
                own[channel, pl.ds(r - TILE, TILE), :] = value

            update_tile(middle, c * per_chunk + j + 1, columns, write)
            return inner_carry

        lax.fori_loop(0, per_chunk, one, 0)
        save(c, 0).start()

        @pl.when(me == 0)
        def _():
            part = pl.ds(pl.multiple_of(c * chunk_rows, TILE), chunk_rows)
            for k in range(channels):
                control[k, part, :] = own[k, part, :]
            pass_on(c)

        return carry

    lax.fori_loop(0, chunks, second_step, 0)

    def compare(c, carry):
        @pl.when(me > 0)
        def _():
            cast(c, 0, me).wait_recv()
            pass_on(c)

        save(c, 1).start()

        def one(j, inner_carry):
            r = pl.multiple_of(c * chunk_rows + j * TILE, TILE)
            total = None
            for k in range(channels):
                d = own[k, pl.ds(r, TILE), :] - control[k, pl.ds(r, TILE), :]
                total = d * d if total is None else total + d * d
            add_regions(squares, r, field[OCEAN, pl.ds(r + TILE, TILE), 0:columns] * total)
            return inner_carry

        lax.fori_loop(0, per_chunk, one, 0)
        return carry

    lax.fori_loop(0, chunks, compare, 0)
    share(squares, 1)
    count_sum = collect(0)

    def finish(c, carry):
        save(c, 0).wait()
        save(c, 1).wait()

        @pl.when(has_next)
        def _():
            cast(c, 1, me + 2).wait_send()

        @pl.when(has_pair)
        def _():
            cast(c, 0, me + 1).wait_send()

        return carry

    lax.fori_loop(0, chunks, finish, 0)
    square_sum = collect(1)
    growth = jnp.sqrt(square_sum / (count_sum * channels) + epsilon)
    growth_out[...] = jnp.broadcast_to(growth, growth_out.shape)


def breed_kernel(target, region, own, control, growth_in, bred, growth):
    regions = growth_in.shape[0]
    channels, rows, columns = own.shape
    ids = region[...]
    factor = jnp.zeros(ids.shape, jnp.float32)
    for k in range(regions):
        value = target[k] / growth_in[k : k + 1, :]
        value = jnp.concatenate([value] * (columns // LANES), axis=1)
        factor = jnp.where(ids == k, jnp.broadcast_to(value, ids.shape), factor)
    for k in range(channels):
        base = control[k]
        bred[k] = base + factor * (own[k] - base)
    shape = growth_in.shape
    diagonal = lax.broadcasted_iota(jnp.int32, shape, 0) == lax.broadcasted_iota(jnp.int32, shape, 1)
    line = jnp.sum(jnp.where(diagonal, growth_in[...], 0.0), axis=0, keepdims=True)
    growth[...] = line[:, 0 : growth.shape[1]]


def per_device(
    sizes, member_state, column_depth, rotation, diffusivity, ocean_mask, region_id, target_rms
):
    members, lons, lats = sizes
    _, channels, rows, columns = member_state.shape
    regions = target_rms.shape[0]
    fields = channels + 3 + LEV
    tall, wide = rows + 2 * TILE, columns + LANES
    chunks = rows // (chunk_tiles(rows) * TILE)
    group = lons * lats
    f32 = jnp.float32
    anywhere = pl.BlockSpec(memory_space=pl.ANY)
    own, control, growth_wide = pl.pallas_call(
        functools.partial(cycle_kernel, sizes),
        out_shape=(
            jax.ShapeDtypeStruct((channels, rows, columns), f32),
            jax.ShapeDtypeStruct((channels, rows, columns), f32),
            jax.ShapeDtypeStruct((regions, LANES), f32),
        ),
        in_specs=[anywhere] * 6,
        out_specs=(anywhere, anywhere, pl.BlockSpec(memory_space=pltpu.VMEM)),
        scratch_shapes=[
            pltpu.VMEM((fields, tall, wide), f32),
            pltpu.VMEM((channels, tall, wide), f32),
            pltpu.VMEM((channels, rows, columns), f32),
            pltpu.VMEM((channels, rows, columns), f32),
            pltpu.VMEM((rows, columns), jnp.int32),
            pltpu.VMEM((rows, columns), jnp.int32),
            pltpu.VMEM((tall, wide), f32),
            pltpu.VMEM((tall, wide), f32),
            pltpu.VMEM((rows, LANES), f32),
            pltpu.VMEM((rows, LANES), f32),
            pltpu.VMEM((tall, LANES), f32),
            pltpu.VMEM((tall, LANES), f32),
            pltpu.VMEM((fields // 2, TILE, columns), f32),
            pltpu.VMEM((fields // 2, TILE, columns), f32),
            pltpu.VMEM((fields // 2, TILE, columns), f32),
            pltpu.VMEM((fields // 2, TILE, columns), f32),
            pltpu.VMEM((regions, TILE, LANES), f32),
            pltpu.VMEM((regions, TILE, LANES), f32),
            pltpu.VMEM((2, group, regions, LANES), f32),
            pltpu.SemaphoreType.DMA((6,)),
            pltpu.SemaphoreType.DMA((8,)),
            pltpu.SemaphoreType.DMA((8,)),
            pltpu.SemaphoreType.DMA((2, chunks)),
            pltpu.SemaphoreType.DMA((chunks,)),
            pltpu.SemaphoreType.DMA((2, chunks)),
            pltpu.SemaphoreType.DMA((2, group - 1)),
            pltpu.SemaphoreType.DMA((2, group - 1)),
        ],
        compiler_params=pltpu.CompilerParams(collective_id=0, has_side_effects=True),
    )(
        member_state.reshape(channels, rows, columns),
        column_depth, rotation, diffusivity, ocean_mask, region_id,
    )
    block = 32 if rows % 32 == 0 else rows
    volume = pl.BlockSpec((channels, block, columns), lambda i: (0, i, 0))
    bred, growth = pl.pallas_call(
        breed_kernel,
        grid=(rows // block,),
        out_shape=(
            jax.ShapeDtypeStruct((channels, rows, columns), f32),
            jax.ShapeDtypeStruct((1, regions), f32),
        ),
        in_specs=[
            pl.BlockSpec(memory_space=pltpu.SMEM),
            pl.BlockSpec((block, columns), lambda i: (i, 0)),
            volume,
            volume,
            pl.BlockSpec((regions, LANES), lambda i: (0, 0)),
        ],
        out_specs=(volume, pl.BlockSpec((1, regions), lambda i: (0, 0))),
    )(target_rms, region_id, own, control, growth_wide)
    return (bred[None], growth)


def solution(mesh):
    sizes = (mesh.shape["member"], mesh.shape["lon"], mesh.shape["lat"])
    return jax.shard_map(
        functools.partial(per_device, sizes),
        mesh=mesh,
        in_specs=(
            P("member", None, "lat", "lon"),
            P("lat", "lon"),
            P("lat", "lon"),
            P(None, "lat", "lon"),
            P("lat", "lon"),
            P("lat", "lon"),
            P(),
        ),
        out_specs=(P("member", None, "lat", "lon"), P("member", None)),
        check_vma=False,
    )
```

time: 187 us -> 71.8 us (0.38)
  the two profiles are of different devices: /device:TPU:0 before, /device:TPU:5 now
where the time goes in v1:
time: 71.8 us; the launch traced here: 71.6 us
  Pallas kernels  71 us (99%)
    pallas_call x1, Pallas kernels, per_device(): pl.pallas_call(functools.partial(cycle_kernel, sizes), out_shape=(jax.Sha...  65.8 us
    pallas_call x1, Pallas kernels, per_device(): pl.pallas_call(breed_kernel, grid=(rows // block,), out_shape=(jax.ShapeD...  5.16 us

profile of v1, /device:TPU:5, one launch (start us, length us, event | category | flops | bytes accessed | tf_op | source)
XLA Modules:
  0.0 71.6 jit_solution(6446530855801783386)
XLA Ops:
  0.6 65.8 %shard_map.86 = (f32[16,128,384]{2,1,0:T(8,128)}, f32[16,128,384]{2,1,0:T(8,128)}, f32[16,128]{1,0:T(8,128)}) custom-call(f32[16,128,384]{2,1,0:T(8,128)} %bitcast.2, f32[128,384]{1,0:T(8,128)} %depth_in.1, f32[128,384]{1,0:T(8,128)} %rotation_in.1, f32[5,128,384]{2,1,0:T(8,128)} %diffusivity_in.1, s32[128,384]{1,0:T(8,128)} %mask_in.1, s32[128,384]{1,0:T(8,128)} %region.1), custom_call_target="tpu_custom_call" | custom-call | tf_op jit(solution)/shard_map/pallas_call | solution.py:503
  66.4 5.2 %shard_map.87 = (f32[16,128,384]{2,1,0:T(8,128)}, f32[1,16]{1,0:T(1,128)}) custom-call(f32[16]{0:T(128)} %target.1, s32[128,384]{1,0:T(8,128)} %region.1, f32[16,128,384]{2,1,0:T(8,128)} %get-tuple-element.7.own, f32[16,128,384]{2,1,0:T(8,128)} %get-tuple-element.8.control, f32[16,128]{1,0:T(8,128)} %get-tuple-element.9.growth_in), custom_call_target="tpu_custom_call" | custom-call | tf_op jit(solution)/shard_map/pallas_call | solution.py:548

commit v2 on v1

--- a/solution.py
+++ b/solution.py
@@ -12,6 +12,7 @@
 MARGIN = 2 * STEPS
 TILE = 8
 LANES = 128
+EARLY = 6
 
 divergence_gain = 0.25
 pressure_gain = 0.25
@@ -22,20 +23,18 @@
 MESH = pl.DeviceIdType.MESH
 
 
-def chunk_tiles(rows):
-    tiles = rows // TILE
-    return 2 if tiles % 2 == 0 else 1
-
-
 def cycle_kernel(
     sizes,
     state_in, depth_in, rotation_in, diffusivity_in, mask_in, region_in,
     own_out, control_out, growth_out,
-    field, middle, own, control, mask, region, surface, merid_sum,
+    field, middle, raw, own, control, mask, region,
+    surface_one, surface_two, merid_one, merid_two,
     send_east, send_west, from_east, from_west,
     send_north, send_south, from_north, from_south,
+    raw_east, raw_west, raw_north, raw_south,
     squares, counts, gathered,
-    in_sem, halo_send, halo_recv, cast_send, cast_recv, out_sem, sum_send, sum_recv,
+    in_sem, halo_send, halo_recv, raw_send, raw_recv, rim_send, rim_recv,
+    cast_send, cast_recv, out_sem, sum_send, sum_recv,
 ):
     members, lons, lats = sizes
     channels, rows, columns = state_in.shape
@@ -43,9 +42,7 @@
     fields = field.shape[0]
     wide = columns + LANES
     tiles = rows // TILE
-    per_chunk = chunk_tiles(rows)
-    chunk_rows = per_chunk * TILE
-    chunks = rows // chunk_rows
+    tall_tiles = tiles + 2
     DEPTH, ROT, OCEAN, DIFF = channels, channels + 1, channels + 2, channels + 3
 
     me = lax.axis_index("member")
@@ -93,6 +90,29 @@
 
     for load in loads:
         load.wait()
+
+    early = min(EARLY, tiles)
+
+    def cells(ref, t):
+        return ref.at[0:channels, pl.ds(pl.multiple_of((t + 1) * TILE, TILE), TILE), 0:columns]
+
+    def hand_down(src, t):
+        return pltpu.make_async_remote_copy(
+            src_ref=cells(src, t), dst_ref=cells(raw, t),
+            send_sem=raw_send.at[t], recv_sem=raw_recv.at[t],
+            device_id=to_member(me + 2), device_id_type=MESH,
+        )
+
+    def hand_down_some(begin, end):
+        @pl.when((me == 0) & has_next)
+        def _():
+            def body(t, carry):
+                hand_down(field, t).start()
+                return carry
+
+            lax.fori_loop(begin, end, body, 0)
+
+    hand_down_some(0, early)
 
     lane = lax.broadcasted_iota(jnp.int32, (TILE, LANES), 1)
     sub = lax.broadcasted_iota(jnp.int32, (TILE, columns), 0)
@@ -255,24 +275,59 @@
         from_east[first, :] = zero_tile
         from_west[first, :] = zero_tile
 
-    for k in range(fields // 2):
-        a, b = 2 * k, 2 * k + 1
-        field[a, first, 0:columns] = pltpu.roll(from_south[k], TILE // 2, 0)
-        field[b, first, 0:columns] = from_south[k]
-        field[a, above, 0:columns] = from_north[k]
-        field[b, above, 0:columns] = pltpu.roll(from_north[k], TILE // 2, 0)
-
-    def unpack(t, carry):
+    pairs = channels // 2
+
+    def rims(east, west, above_rows, below_rows):
+        def rim(src, dst, index):
+            return pltpu.make_async_remote_copy(
+                src_ref=src, dst_ref=dst, send_sem=rim_send.at[index], recv_sem=rim_recv.at[index],
+                device_id=to_member(me + 2), device_id_type=MESH,
+            )
+
+        return (
+            rim(east, raw_east, 0),
+            rim(west, raw_west, 1),
+            rim(above_rows, raw_north, 2),
+            rim(below_rows, raw_south, 3),
+        )
+
+    own_rims = rims(from_east, from_west, from_north.at[0:pairs], from_south.at[0:pairs])
+    raw_rims = rims(raw_east, raw_west, raw_north, raw_south)
+
+    def start_rims(copies):
+        copies[0].start()
+        copies[1].start()
+
+        @pl.when(has_north)
+        def _():
+            copies[2].start()
+
+        @pl.when(has_south)
+        def _():
+            copies[3].start()
+
+    @pl.when((me == 0) & has_next)
+    def _():
+        start_rims(own_rims)
+
+    hand_down_some(early, tiles)
+
+    def edge_rows(ref, above_rows, below_rows, count):
+        for k in range(count):
+            a, b = 2 * k, 2 * k + 1
+            ref[a, first, 0:columns] = pltpu.roll(below_rows[k], TILE // 2, 0)
+            ref[b, first, 0:columns] = below_rows[k]
+            ref[a, above, 0:columns] = above_rows[k]
+            ref[b, above, 0:columns] = pltpu.roll(above_rows[k], TILE // 2, 0)
+
+    def edge_columns(ref, east_ref, west_ref, count, t):
         r = pl.multiple_of(t * TILE, TILE)
-        east = from_east[pl.ds(r, TILE), :]
-        west = from_west[pl.ds(r, TILE), :]
-        for f in range(fields):
+        east = east_ref[pl.ds(r, TILE), :]
+        west = west_ref[pl.ds(r, TILE), :]
+        for f in range(count):
             to_first = pltpu.roll(east, LANES - MARGIN * f, 1) if f else east
             to_last = pltpu.roll(west, LANES - MARGIN - MARGIN * f, 1)
-            field[f, pl.ds(r, TILE), columns:wide] = jnp.where(lane < MARGIN, to_first, to_last)
-        return carry
-
-    lax.fori_loop(0, tiles + 2, unpack, 0)
+            ref[f, pl.ds(r, TILE), columns:wide] = jnp.where(lane < MARGIN, to_first, to_last)
 
     sub_wide = lax.broadcasted_iota(jnp.int32, (TILE, wide), 0)
 
@@ -301,33 +356,23 @@
             total = total + ref[base + k, pl.ds(r, TILE), :]
         return total
 
-    def merid_pass(src):
-        def body(t, carry):
-            r = pl.multiple_of(t * TILE, TILE)
-            merid_sum[pl.ds(r, TILE), :] = add_up(src, 1 + LEV, r)
-            return carry
-
-        lax.fori_loop(0, tiles + 2, body, 0)
-
-    def surface_pass(src):
-        def body(t, carry):
-            r, before, after = starts(t)
-            e, w = east_west(add_up(src, 1, r), wide)
-            n, s = north_south(
-                merid_sum[pl.ds(r, TILE), :],
-                merid_sum[pl.ds(before, TILE), :],
-                merid_sum[pl.ds(after, TILE), :],
-            )
-            divergence = (e - w) + (n - s)
-            now = pl.ds(r, TILE)
-            surface[now, :] = field[OCEAN, now, :] * (
-                src[0, now, :] - (divergence_gain / LEV) * field[DEPTH, now, :] * divergence
-            )
-            return carry
-
-        lax.fori_loop(0, tiles + 2, body, 0)
-
-    def update_tile(src, t, width, write):
+    def merid_tile(src, merid, t):
+        r = pl.multiple_of(t * TILE, TILE)
+        merid[pl.ds(r, TILE), :] = add_up(src, 1 + LEV, r)
+
+    def surface_tile(src, merid, surface, t):
+        r, before, after = starts(t)
+        e, w = east_west(add_up(src, 1, r), wide)
+        n, s = north_south(
+            merid[pl.ds(r, TILE), :], merid[pl.ds(before, TILE), :], merid[pl.ds(after, TILE), :]
+        )
+        divergence = (e - w) + (n - s)
+        now = pl.ds(r, TILE)
+        surface[now, :] = field[OCEAN, now, :] * (
+            src[0, now, :] - (divergence_gain / LEV) * field[DEPTH, now, :] * divergence
+        )
+
+    def update_tile(src, surface, t, width, write):
         r, before, after = starts(t)
         now, below, beyond = pl.ds(r, TILE), pl.ds(before, TILE), pl.ds(after, TILE)
 
@@ -369,102 +414,167 @@
             write(1 + LEV + k, r, new_v)
             write(1 + 2 * LEV + k, r, new_c)
 
-    merid_pass(field)
-    surface_pass(field)
-
-    def first_step(t, carry):
-        def write(channel, r, value):
+    def run_steps(src, east, west, count, dst, arrive, leave):
+        def middle_write(channel, r, value):
             middle[channel, pl.ds(r, TILE), :] = value
 
-        update_tile(field, t, wide, write)
-        return carry
-
-    lax.fori_loop(0, tiles + 2, first_step, 0)
-    merid_pass(middle)
-    surface_pass(middle)
-
-    def cast(c, which, device):
-        part = control.at[:, pl.ds(pl.multiple_of(c * chunk_rows, TILE), chunk_rows), :]
+        def last_write(channel, r, value):
+            dst[channel, pl.ds(r - TILE, TILE), :] = value
+
+        def body(i, carry):
+            @pl.when(i < tall_tiles)
+            def _():
+                @pl.when((i >= 1) & (i <= tiles))
+                def _():
+                    arrive(i - 1)
+
+                edge_columns(src, east, west, count, i)
+                merid_tile(src, merid_one, i)
+
+            @pl.when((i >= 1) & (i <= tall_tiles))
+            def _():
+                surface_tile(src, merid_one, surface_one, i - 1)
+
+            @pl.when((i >= 2) & (i <= tall_tiles + 1))
+            def _():
+                update_tile(src, surface_one, i - 2, wide, middle_write)
+                merid_tile(middle, merid_two, i - 2)
+
+            @pl.when((i >= 3) & (i <= tall_tiles + 2))
+            def _():
+                surface_tile(middle, merid_two, surface_two, i - 3)
+
+            @pl.when(i >= 5)
+            def _():
+                update_tile(middle, surface_two, i - 4, columns, last_write)
+                leave(i - 5)
+
+            return carry
+
+        lax.fori_loop(0, tall_tiles + 3, body, 0)
+
+    def part(t):
+        return pl.ds(pl.multiple_of(t * TILE, TILE), TILE)
+
+    def to_pair(t):
         return pltpu.make_async_remote_copy(
-            src_ref=part, dst_ref=part, send_sem=cast_send.at[which, c], recv_sem=cast_recv.at[c],
-            device_id=to_member(device), device_id_type=MESH,
-        )
-
-    def pass_on(c):
+            src_ref=control.at[:, part(t), :], dst_ref=control.at[:, part(t), :],
+            send_sem=cast_send.at[t], recv_sem=cast_recv.at[t],
+            device_id=to_member(me + 1), device_id_type=MESH,
+        )
+
+    def save(t, which):
+        src, dst = (own, own_out) if which == 0 else (control, control_out)
+        return pltpu.make_async_copy(src.at[:, part(t), :], dst.at[:, part(t), :], out_sem.at[which, t])
+
+    def control_done(t):
+        @pl.when(has_pair)
+        def _():
+            to_pair(t).start()
+
+        save(t, 1).start()
+
+    def compare(t):
+        total = None
+        for k in range(channels):
+            d = own[k, part(t), :] - control[k, part(t), :]
+            total = d * d if total is None else total + d * d
+        r = pl.multiple_of(t * TILE, TILE)
+        add_regions(squares, r, field[OCEAN, pl.ds(r + TILE, TILE), 0:columns] * total)
+
+    def own_leave(t):
+        save(t, 0).start()
+
+        @pl.when(me == 0)
+        def _():
+            for k in range(channels):
+                control[k, part(t), :] = own[k, part(t), :]
+            control_done(t)
+
+    edge_rows(field, from_north, from_south, fields // 2)
+    run_steps(field, from_east, from_west, fields, own, lambda t: None, own_leave)
+
+    @pl.when(even & (me > 0))
+    def _():
+        raw_rims[0].wait_recv()
+        raw_rims[1].wait_recv()
+
+        @pl.when(has_north)
+        def _():
+            raw_rims[2].wait_recv()
+
+        @pl.when(has_south)
+        def _():
+            raw_rims[3].wait_recv()
+
         @pl.when(has_next)
         def _():
-            cast(c, 1, me + 2).start()
-
-        @pl.when(has_pair)
-        def _():
-            cast(c, 0, me + 1).start()
-
-    def save(c, which):
-        part = pl.ds(pl.multiple_of(c * chunk_rows, TILE), chunk_rows)
-        src, dst = (own, own_out) if which == 0 else (control, control_out)
-        return pltpu.make_async_copy(src.at[:, part, :], dst.at[:, part, :], out_sem.at[which, c])
-
-    def second_step(c, carry):
-        def one(j, inner_carry):
-            def write(channel, r, value):
-                own[channel, pl.ds(r - TILE, TILE), :] = value
-
-            update_tile(middle, c * per_chunk + j + 1, columns, write)
-            return inner_carry
-
-        lax.fori_loop(0, per_chunk, one, 0)
-        save(c, 0).start()
-
-        @pl.when(me == 0)
-        def _():
-            part = pl.ds(pl.multiple_of(c * chunk_rows, TILE), chunk_rows)
-            for k in range(channels):
-                control[k, part, :] = own[k, part, :]
-            pass_on(c)
-
-        return carry
-
-    lax.fori_loop(0, chunks, second_step, 0)
-
-    def compare(c, carry):
-        @pl.when(me > 0)
-        def _():
-            cast(c, 0, me).wait_recv()
-            pass_on(c)
-
-        save(c, 1).start()
-
-        def one(j, inner_carry):
-            r = pl.multiple_of(c * chunk_rows + j * TILE, TILE)
-            total = None
-            for k in range(channels):
-                d = own[k, pl.ds(r, TILE), :] - control[k, pl.ds(r, TILE), :]
-                total = d * d if total is None else total + d * d
-            add_regions(squares, r, field[OCEAN, pl.ds(r + TILE, TILE), 0:columns] * total)
-            return inner_carry
-
-        lax.fori_loop(0, per_chunk, one, 0)
-        return carry
-
-    lax.fori_loop(0, chunks, compare, 0)
+            start_rims(raw_rims)
+
+        @pl.when(jnp.logical_not(has_north))
+        def _():
+            raw_north[...] = jnp.zeros_like(raw_north)
+
+        @pl.when(jnp.logical_not(has_south))
+        def _():
+            raw_south[...] = jnp.zeros_like(raw_south)
+
+        edge_rows(raw, raw_north, raw_south, pairs)
+
+        def arrive(t):
+            hand_down(raw, t).wait_recv()
+
+            @pl.when(has_next)
+            def _():
+                hand_down(raw, t).start()
+
+        def leave(t):
+            control_done(t)
+            compare(t)
+
+        run_steps(raw, raw_east, raw_west, channels, control, arrive, leave)
+
+    @pl.when(jnp.logical_not(even))
+    def _():
+        def body(t, carry):
+            to_pair(t).wait_recv()
+            save(t, 1).start()
+            compare(t)
+            return carry
+
+        lax.fori_loop(0, tiles, body, 0)
+
     share(squares, 1)
     count_sum = collect(0)
 
-    def finish(c, carry):
-        save(c, 0).wait()
-        save(c, 1).wait()
+    @pl.when(has_next)
+    def _():
+        for copy in raw_rims[0:2]:
+            copy.wait_send()
+
+        @pl.when(has_north)
+        def _():
+            raw_rims[2].wait_send()
+
+        @pl.when(has_south)
+        def _():
+            raw_rims[3].wait_send()
+
+    def finish(t, carry):
+        save(t, 0).wait()
+        save(t, 1).wait()
 
         @pl.when(has_next)
         def _():
-            cast(c, 1, me + 2).wait_send()
+            hand_down(raw, t).wait_send()
 
         @pl.when(has_pair)
         def _():
-            cast(c, 0, me + 1).wait_send()
+            to_pair(t).wait_send()
 
         return carry
 
-    lax.fori_loop(0, chunks, finish, 0)
+    lax.fori_loop(0, tiles, finish, 0)
     square_sum = collect(1)
     growth = jnp.sqrt(square_sum / (count_sum * channels) + epsilon)
     growth_out[...] = jnp.broadcast_to(growth, growth_out.shape)
@@ -496,7 +606,7 @@
     regions = target_rms.shape[0]
     fields = channels + 3 + LEV
     tall, wide = rows + 2 * TILE, columns + LANES
-    chunks = rows // (chunk_tiles(rows) * TILE)
+    tiles = rows // TILE
     group = lons * lats
     f32 = jnp.float32
     anywhere = pl.BlockSpec(memory_space=pl.ANY)
@@ -512,10 +622,13 @@
         scratch_shapes=[
             pltpu.VMEM((fields, tall, wide), f32),
             pltpu.VMEM((channels, tall, wide), f32),
+            pltpu.VMEM((channels, tall, wide), f32),
             pltpu.VMEM((channels, rows, columns), f32),
             pltpu.VMEM((channels, rows, columns), f32),
             pltpu.VMEM((rows, columns), jnp.int32),
             pltpu.VMEM((rows, columns), jnp.int32),
+            pltpu.VMEM((tall, wide), f32),
+            pltpu.VMEM((tall, wide), f32),
             pltpu.VMEM((tall, wide), f32),
             pltpu.VMEM((tall, wide), f32),
             pltpu.VMEM((rows, LANES), f32),
@@ -526,15 +639,23 @@
             pltpu.VMEM((fields // 2, TILE, columns), f32),
             pltpu.VMEM((fields // 2, TILE, columns), f32),
             pltpu.VMEM((fields // 2, TILE, columns), f32),
+            pltpu.VMEM((tall, LANES), f32),
+            pltpu.VMEM((tall, LANES), f32),
+            pltpu.VMEM((channels // 2, TILE, columns), f32),
+            pltpu.VMEM((channels // 2, TILE, columns), f32),
             pltpu.VMEM((regions, TILE, LANES), f32),
             pltpu.VMEM((regions, TILE, LANES), f32),
             pltpu.VMEM((2, group, regions, LANES), f32),
             pltpu.SemaphoreType.DMA((6,)),
             pltpu.SemaphoreType.DMA((8,)),
             pltpu.SemaphoreType.DMA((8,)),
-            pltpu.SemaphoreType.DMA((2, chunks)),
-            pltpu.SemaphoreType.DMA((chunks,)),
-            pltpu.SemaphoreType.DMA((2, chunks)),
+            pltpu.SemaphoreType.DMA((tiles,)),
+            pltpu.SemaphoreType.DMA((tiles,)),
+            pltpu.SemaphoreType.DMA((4,)),
+            pltpu.SemaphoreType.DMA((4,)),
+            pltpu.SemaphoreType.DMA((tiles,)),
+            pltpu.SemaphoreType.DMA((tiles,)),
+            pltpu.SemaphoreType.DMA((2, tiles)),
             pltpu.SemaphoreType.DMA((2, group - 1)),
             pltpu.SemaphoreType.DMA((2, group - 1)),
         ],

time: 71.8 us -> 59.2 us (0.82)
  Pallas kernels: 71 us -> 58.4 us
    pallas_call x1, Pallas kernels: 65.8 us -> 53.2 us  [per_device(): pl.pallas_call(functools.partial(cycle_kernel, sizes), out_shape=(jax.Sha...]
where the time goes in v2:
time: 59.2 us; the launch traced here: 59 us
  Pallas kernels  58.4 us (99%)
  between operations  0.64 us (1%)
    pallas_call x1, Pallas kernels, per_device(): pl.pallas_call(functools.partial(cycle_kernel, sizes), out_shape=(jax.Sha...  53.2 us
    pallas_call x1, Pallas kernels, per_device(): pl.pallas_call(breed_kernel, grid=(rows // block,), out_shape=(jax.ShapeD...  5.16 us

profile of v2, /device:TPU:5, one launch (start us, length us, event | category | flops | bytes accessed | tf_op | source)
XLA Modules:
  0.0 59.0 jit_solution(1915810388801550512)
XLA Ops:
  0.6 53.2 %shard_map.86 = (f32[16,128,384]{2,1,0:T(8,128)}, f32[16,128,384]{2,1,0:T(8,128)}, f32[16,128]{1,0:T(8,128)}) custom-call(f32[16,128,384]{2,1,0:T(8,128)} %bitcast.2, f32[128,384]{1,0:T(8,128)} %depth_in.1, f32[128,384]{1,0:T(8,128)} %rotation_in.1, f32[5,128,384]{2,1,0:T(8,128)} %diffusivity_in.1, s32[128,384]{1,0:T(8,128)} %mask_in.1, s32[128,384]{1,0:T(8,128)} %region.1), custom_call_target="tpu_custom_call" | custom-call | tf_op jit(solution)/shard_map/pallas_call | solution.py:613
  53.9 5.2 %shard_map.87 = (f32[16,128,384]{2,1,0:T(8,128)}, f32[1,16]{1,0:T(1,128)}) custom-call(f32[16]{0:T(128)} %target.1, s32[128,384]{1,0:T(8,128)} %region.1, f32[16,128,384]{2,1,0:T(8,128)} %get-tuple-element.7.own, f32[16,128,384]{2,1,0:T(8,128)} %get-tuple-element.8.control, f32[16,128]{1,0:T(8,128)} %get-tuple-element.9.growth_in), custom_call_target="tpu_custom_call" | custom-call | tf_op jit(solution)/shard_map/pallas_call | solution.py:669

commit v3 on v2

--- a/solution.py
+++ b/solution.py
@@ -12,7 +12,9 @@
 MARGIN = 2 * STEPS
 TILE = 8
 LANES = 128
-EARLY = 6
+EARLY = 9
+KERNEL_BYTES = 56 * 2**20
+BREED_BYTES = 16 * 2**20
 
 divergence_gain = 0.25
 pressure_gain = 0.25
@@ -26,15 +28,15 @@
 def cycle_kernel(
     sizes,
     state_in, depth_in, rotation_in, diffusivity_in, mask_in, region_in,
-    own_out, control_out, growth_out,
-    field, middle, raw, own, control, mask, region,
+    own, control, growth_out,
+    field, middle, raw, mask, region,
     surface_one, surface_two, merid_one, merid_two,
     send_east, send_west, from_east, from_west,
     send_north, send_south, from_north, from_south,
     raw_east, raw_west, raw_north, raw_south,
     squares, counts, gathered,
     in_sem, halo_send, halo_recv, raw_send, raw_recv, rim_send, rim_recv,
-    cast_send, cast_recv, out_sem, sum_send, sum_recv,
+    cast_send, cast_recv, sum_send, sum_recv,
 ):
     members, lons, lats = sizes
     channels, rows, columns = state_in.shape
@@ -463,16 +465,10 @@
             device_id=to_member(me + 1), device_id_type=MESH,
         )
 
-    def save(t, which):
-        src, dst = (own, own_out) if which == 0 else (control, control_out)
-        return pltpu.make_async_copy(src.at[:, part(t), :], dst.at[:, part(t), :], out_sem.at[which, t])
-
     def control_done(t):
         @pl.when(has_pair)
         def _():
             to_pair(t).start()
-
-        save(t, 1).start()
 
     def compare(t):
         total = None
@@ -483,8 +479,6 @@
         add_regions(squares, r, field[OCEAN, pl.ds(r + TILE, TILE), 0:columns] * total)
 
     def own_leave(t):
-        save(t, 0).start()
-
         @pl.when(me == 0)
         def _():
             for k in range(channels):
@@ -538,7 +532,6 @@
     def _():
         def body(t, carry):
             to_pair(t).wait_recv()
-            save(t, 1).start()
             compare(t)
             return carry
 
@@ -561,9 +554,6 @@
             raw_rims[3].wait_send()
 
     def finish(t, carry):
-        save(t, 0).wait()
-        save(t, 1).wait()
-
         @pl.when(has_next)
         def _():
             hand_down(raw, t).wait_send()
@@ -582,7 +572,8 @@
 
 def breed_kernel(target, region, own, control, growth_in, bred, growth):
     regions = growth_in.shape[0]
-    channels, rows, columns = own.shape
+    channels, block, columns = bred.shape
+    now = pl.ds(pl.multiple_of(pl.program_id(0) * block, TILE), block)
     ids = region[...]
     factor = jnp.zeros(ids.shape, jnp.float32)
     for k in range(regions):
@@ -590,8 +581,8 @@
         value = jnp.concatenate([value] * (columns // LANES), axis=1)
         factor = jnp.where(ids == k, jnp.broadcast_to(value, ids.shape), factor)
     for k in range(channels):
-        base = control[k]
-        bred[k] = base + factor * (own[k] - base)
+        base = control[k, now, :]
+        bred[k] = base + factor * (own[k, now, :] - base)
     shape = growth_in.shape
     diagonal = lax.broadcasted_iota(jnp.int32, shape, 0) == lax.broadcasted_iota(jnp.int32, shape, 1)
     line = jnp.sum(jnp.where(diagonal, growth_in[...], 0.0), axis=0, keepdims=True)
@@ -610,21 +601,20 @@
     group = lons * lats
     f32 = jnp.float32
     anywhere = pl.BlockSpec(memory_space=pl.ANY)
+    resident = pl.BlockSpec(memory_space=pltpu.VMEM)
     own, control, growth_wide = pl.pallas_call(
         functools.partial(cycle_kernel, sizes),
         out_shape=(
-            jax.ShapeDtypeStruct((channels, rows, columns), f32),
-            jax.ShapeDtypeStruct((channels, rows, columns), f32),
-            jax.ShapeDtypeStruct((regions, LANES), f32),
+            pltpu.VMEM((channels, rows, columns), f32),
+            pltpu.VMEM((channels, rows, columns), f32),
+            pltpu.VMEM((regions, LANES), f32),
         ),
         in_specs=[anywhere] * 6,
-        out_specs=(anywhere, anywhere, pl.BlockSpec(memory_space=pltpu.VMEM)),
+        out_specs=(resident,) * 3,
         scratch_shapes=[
             pltpu.VMEM((fields, tall, wide), f32),
             pltpu.VMEM((channels, tall, wide), f32),
             pltpu.VMEM((channels, tall, wide), f32),
-            pltpu.VMEM((channels, rows, columns), f32),
-            pltpu.VMEM((channels, rows, columns), f32),
             pltpu.VMEM((rows, columns), jnp.int32),
             pltpu.VMEM((rows, columns), jnp.int32),
             pltpu.VMEM((tall, wide), f32),
@@ -655,17 +645,17 @@
             pltpu.SemaphoreType.DMA((4,)),
             pltpu.SemaphoreType.DMA((tiles,)),
             pltpu.SemaphoreType.DMA((tiles,)),
-            pltpu.SemaphoreType.DMA((2, tiles)),
             pltpu.SemaphoreType.DMA((2, group - 1)),
             pltpu.SemaphoreType.DMA((2, group - 1)),
         ],
-        compiler_params=pltpu.CompilerParams(collective_id=0, has_side_effects=True),
+        compiler_params=pltpu.CompilerParams(
+            collective_id=0, has_side_effects=True, vmem_limit_bytes=KERNEL_BYTES
+        ),
     )(
         member_state.reshape(channels, rows, columns),
         column_depth, rotation, diffusivity, ocean_mask, region_id,
     )
-    block = 32 if rows % 32 == 0 else rows
-    volume = pl.BlockSpec((channels, block, columns), lambda i: (0, i, 0))
+    block = 2 * TILE if rows % (2 * TILE) == 0 else TILE
     bred, growth = pl.pallas_call(
         breed_kernel,
         grid=(rows // block,),
@@ -676,11 +666,15 @@
         in_specs=[
             pl.BlockSpec(memory_space=pltpu.SMEM),
             pl.BlockSpec((block, columns), lambda i: (i, 0)),
-            volume,
-            volume,
-            pl.BlockSpec((regions, LANES), lambda i: (0, 0)),
+            resident,
+            resident,
+            resident,
         ],
-        out_specs=(volume, pl.BlockSpec((1, regions), lambda i: (0, 0))),
+        out_specs=(
+            pl.BlockSpec((channels, block, columns), lambda i: (0, i, 0)),
+            pl.BlockSpec((1, regions), lambda i: (0, 0)),
+        ),
+        compiler_params=pltpu.CompilerParams(vmem_limit_bytes=BREED_BYTES),
     )(target_rms, region_id, own, control, growth_wide)
     return (bred[None], growth)
 

time: 59.2 us -> 57.3 us (0.968)
  Pallas kernels: 58.4 us -> 56.5 us
    pallas_call x1, Pallas kernels: 5.16 us -> 4.05 us  [per_device(): pl.pallas_call(breed_kernel, grid=(rows // block,), out_shape=(jax.ShapeD...]
    pallas_call x1, Pallas kernels: 53.2 us -> 52.4 us  [per_device(): pl.pallas_call(functools.partial(cycle_kernel, sizes), out_shape=(pltpu.V...]
where the time goes in v3:
time: 57.3 us; the launch traced here: 57.1 us
  Pallas kernels  56.5 us (99%)
  between operations  0.67 us (1%)
    pallas_call x1, Pallas kernels, per_device(): pl.pallas_call(functools.partial(cycle_kernel, sizes), out_shape=(pltpu.V...  52.4 us
    pallas_call x1, Pallas kernels, per_device(): pl.pallas_call(breed_kernel, grid=(rows // block,), out_shape=(jax.ShapeD...  4.05 us

profile of v3, /device:TPU:5, one launch (start us, length us, event | category | flops | bytes accessed | tf_op | source)
XLA Modules:
  0.0 57.1 jit_solution(4577925442319817446)
XLA Ops:
  0.6 0.0 copy-start
  0.6 0.0 copy-start.1
  0.7 52.4 %shard_map.86 = (f32[16,128,384]{2,1,0:T(8,128)S(1)}, f32[16,128,384]{2,1,0:T(8,128)S(1)}, f32[16,128]{1,0:T(8,128)S(1)}) custom-call(f32[16,128,384]{2,1,0:T(8,128)} %bitcast.2, f32[128,384]{1,0:T(8,128)} %depth_in.1, f32[128,384]{1,0:T(8,128)} %rotation_in.1, f32[5,128,384]{2,1,0:T(8,128)} %diffusivity_in.1, s32[128,384]{1,0:T(8,128)} %mask_in.1, ...), custom_call_target="tpu_custom_call" | custom-call | tf_op jit(solution)/shard_map/pallas_call | solution.py:605
  53.1 0.0 copy-done
  53.1 0.0 copy-done.1
  53.1 4.1 %shard_map.87 = (f32[16,128,384]{2,1,0:T(8,128)}, f32[1,16]{1,0:T(1,128)}) custom-call(f32[16]{0:T(128)S(1)} %copy-done.1, s32[128,384]{1,0:T(8,128)S(1)} %copy-done, f32[16,128,384]{2,1,0:T(8,128)S(1)} %get-tuple-element.7.own, f32[16,128,384]{2,1,0:T(8,128)S(1)} %get-tuple-element.8.control, f32[16,128]{1,0:T(8,128)S(1)} %get-tuple-element.9.growth_in), custom_call_target="tpu_custom_call" | custom-call | tf_op jit(solution)/shard_map/pallas_call | solution.py:659
Async XLA Ops:
  0.6 52.4 %copy-start = (s32[128,384]{1,0:T(8,128)S(1)}, s32[128,384]{1,0:T(8,128)}, u32[]{:S(2)}) copy-start(s32[128,384]{1,0:T(8,128)} %region.1) | copy-start | bytes 589828
  0.6 52.4 %copy-start.1 = (f32[16]{0:T(128)S(1)}, f32[16]{0:T(128)}, u32[]{:S(2)}) copy-start(f32[16]{0:T(128)} %target.1) | copy-start | bytes 196
